TPU v7x, 256 devices: a whole 4x4x8 slice. The times are simulated.
256 devices in a mesh: dp: 32 (over y, z_lo, core), cent: 8 (over x, z_hi).
Axes of the slice: x: 4, y: 4, z: 8 (z_hi: 2, z_lo: 4; z = z_hi * 4 + z_lo), core: 2. Of those that a mesh axis runs over, the one named last changes fastest.
Arguments:
- hidden: bfloat16 [5632, 11008], P('dp', 'cent'), may hold values from -6 to 6
- residual: bfloat16 [5632, 4096], P('dp', 'cent'), may hold values from -6 to 6
- down_weight: bfloat16 [11008, 4096], P('cent', 'dp'), may hold values from -0.0546875 to 0.0546875
- gain: float32 [4096], P('cent'), may hold values from 0.1 to 1.9
- proj_weight: bfloat16 [4096, 1024], P('cent'), may hold values from -0.09375 to 0.09375
- centroids: bfloat16 [131072, 1024], P(('dp', 'cent')), may hold values from -24 to 24
Outputs:
- weighted: float32 [131072, 1024], P(('dp', 'cent'))
- counts: float32 [131072], P(('dp', 'cent'))
All inputs are finite; a program needn't handle non-finite values.
Results may differ from a plain program's by a relative error of at most 0.011.
Values may be sent and summed in bfloat16 or wider, within the bound.
A program may use at most 128 MiB of HBM per device.

v0:
```python
import math
import jax
import jax.numpy as jnp
from jax import lax
from jax.sharding import PartitionSpec as P


def body(hidden, residual, down_weight, gain, proj_weight, centroids):
    partial_layer = jnp.dot(
        hidden,
        lax.all_gather(down_weight, "dp", axis=1, tiled=True),
        preferred_element_type=jnp.float32,
    )
    layer_out = lax.psum_scatter(partial_layer, "cent", scatter_dimension=1, tiled=True)
    normed = ((layer_out + residual.astype(jnp.float32)) * gain).astype(jnp.bfloat16)
    partial_embed = jnp.dot(normed, proj_weight, preferred_element_type=jnp.float32)
    embed_width = proj_weight.shape[1]
    embed_full = lax.psum(partial_embed, "cent")
    scaled = (
        embed_full * lax.rsqrt(jnp.mean(embed_full * embed_full, axis=1, keepdims=True) + 1e-06)
    ).astype(jnp.bfloat16)
    gathered = lax.all_gather(scaled, "dp", axis=0, tiled=True)
    inverse = 1.0 / (math.sqrt(embed_width) * 0.05)
    scores = (
        lax.dot_general(
            gathered, centroids, (((1,), (1,)), ((), ())), preferred_element_type=jnp.float32
        )
        * inverse
    )
    local_max = jnp.max(scores, axis=1)
    row_max = lax.pmax(local_max, ("dp", "cent"))
    row_total = lax.psum(jnp.sum(jnp.exp(scores - row_max[:, None]), axis=1), ("dp", "cent"))
    log_total = row_max + jnp.log(row_total)
    probability = jnp.exp(scores - log_total[:, None])
    scale_up = centroids.shape[0] * lax.axis_size("dp") * lax.axis_size("cent") / gathered.shape[0]
    counts = scale_up * jnp.sum(probability, axis=0)
    prob_low = probability.astype(jnp.bfloat16)
    weighted = scale_up * lax.dot_general(
        prob_low, gathered, (((0,), (0,)), ((), ())), preferred_element_type=jnp.float32
    )
    return (weighted, counts)


def solution(mesh):
    in_specs = (
        P("dp", "cent"),
        P("dp", "cent"),
        P("cent", "dp"),
        P("cent"),
        P("cent", None),
        P(("dp", "cent"), None),
    )
    out_specs = (P(("dp", "cent"), None), P(("dp", "cent")))
    return jax.shard_map(body, mesh=mesh, in_specs=in_specs, out_specs=out_specs, check_vma=False)
```

profile of v0, /device:TPU:1, one launch (start us, length us, event | category | flops | bytes accessed | tf_op | source)
XLA Modules:
  0.0 617.1 jit_solution(13492038344672853306)
XLA Ops:
  7.2 0.0 copy-start
  7.2 0.0 copy-start.1
  7.2 0.0 copy-start.3
  7.2 0.0 copy-start.2
  7.2 0.0 all-gather.3.cloned.1.call-start
  7.3 0.7 all-gather.3.cloned.1.call-update
  7.9 0.0 reduce-scatter.2.cloned.1.call-start
  8.0 105.2 %all-gather.3.cloned.1.call-done = bf16[1376,4096]{1,0:T(8,128)(2,1)} async-done(((bf16[1376,128]{1,0:T(8,128)(2,1)}), bf16[1376,4096]{1,0:T(8,128)(2,1)}) %all-gather.3.cloned.1.call-update) | async-done | bytes 11272208 | tf_op jit(solution)/shard_map/all_gather | solution.py:11
  113.2 8.5 %fusion.11 = f32[176,4096]{1,0:T(8,128)} fusion(bf16[176,1376]{1,0:T(8,128)(2,1)} %param.6, bf16[1376,4096]{1,0:T(8,128)(2,1)} %all-gather.3.cloned.1.call-done), kind=kOutput, calls=%fused_computation.17 | convolution fusion | flops 1983905792 | bytes 14640128 | tf_op jit(solution)/shard_map/dot_general | solution.py:9
  121.7 0.0 reduce-scatter.2.cloned.1.call-update
  121.7 0.0 all-reduce.2.cloned.1.call-start
  121.8 103.8 %reduce-scatter.2.cloned.1.call-done = f32[176,512]{1,0:T(8,128)} async-done(((f32[176,4096]{1,0:T(8,128)}), f32[176,512]{1,0:T(8,128)}) %reduce-scatter.2.cloned.1.call-update) | async-done | bytes 360464 | tf_op jit(solution)/shard_map/reduce_scatter | solution.py:14
  225.6 0.0 copy-done.1
  225.6 0.0 copy-done.3
  225.6 0.0 copy-done.2
  225.6 2.2 fusion.8
  227.8 0.0 all-reduce.2.cloned.1.call-update
  227.8 0.0 all-gather.5.cloned.1.call-start
  227.8 112.2 %all-reduce.2.cloned.1.call-done = f32[176,1024]{1,0:T(8,128)} async-done(((f32[176,1024]{1,0:T(8,128)}), f32[176,1024]{1,0:T(8,128)}) %all-reduce.2.cloned.1.call-update) | async-done | bytes 720912 | tf_op jit(solution)/shard_map/psum | solution.py:18
  340.1 1.2 multiply_reduce_fusion
  341.3 2.0 multiply_convert_fusion
  343.3 0.0 all-gather.5.cloned.1.call-update
  343.3 78.9 %all-gather.5.cloned.1.call-done = bf16[5632,1024]{1,0:T(8,128)(2,1)} async-done(((bf16[176,1024]{1,0:T(8,128)(2,1)}), bf16[5632,1024]{1,0:T(8,128)(2,1)}) %all-gather.5.cloned.1.call-update) | async-done | bytes 11534352 | tf_op jit(solution)/shard_map/all_gather | solution.py:22
  422.2 0.0 copy-done
  422.2 13.2 %fusion.10 = (f32[5632]{0:T(1024)S(1)}, f32[5632,512]{0,1:T(8,128)}) fusion(bf16[5632,1024]{1,0:T(8,128)(2,1)} %all-gather.5.cloned.1.call-done, bf16[512,1024]{1,0:T(8,128)(2,1)S(1)} %copy-done), kind=kOutput, calls=%fused_computation.16 | convolution fusion | flops 5911341568 | bytes 24139776 | tf_op jit(solution)/shard_map/dot_general | solution.py:25
  435.3 76.1 %pmax.7 = f32[5632]{0:T(1024)S(1)} all-reduce(f32[5632]{0:T(1024)S(1)} %get-tuple-element.2), channel_id=1, replica_groups=mesh['dp'=32,'cent'=8] {'dp','cent'}, use_global_device_ids=true, to_apply=%region_4.0 | all-reduce | flops 5632 | bytes 45056 | tf_op jit(solution)/shard_map/pmax | solution.py:31
  511.4 6.0 exponential_reduce_fusion
  517.4 73.3 %psum.15 = f32[5632]{0:T(1024)S(1)} all-reduce(f32[5632]{0:T(1024)S(1)} %exponential_reduce_fusion), channel_id=1, replica_groups=mesh['dp'=32,'cent'=8] {'dp','cent'}, use_global_device_ids=true, to_apply=%region_6.0 | all-reduce | flops 5632 | bytes 45056 | tf_op jit(solution)/shard_map/psum | solution.py:32
  590.7 6.0 fusion
  596.7 0.6 broadcast_multiply_fusion
  597.3 13.3 %fusion.5 = f32[512,1024]{1,0:T(8,128)} fusion(bf16[5632,1024]{1,0:T(8,128)(2,1)} %all-gather.5.cloned.1.call-done, f32[5632,512]{0,1:T(8,128)} %get-tuple-element.3, f32[5632]{0:T(1024)S(1)} %log_add_fusion), kind=kOutput, calls=%fused_computation.7 | convolution fusion | flops 5911871488 | bytes 25188352 | tf_op jit(solution)/shard_map/dot_general | solution.py:38
  (2 shorter events, 0.0 us)
Async XLA Ops:
  7.2 415.0 %copy-start = (bf16[512,1024]{1,0:T(8,128)(2,1)S(1)}, bf16[512,1024]{1,0:T(8,128)(2,1)}, u32[]{:S(2)}) copy-start(bf16[512,1024]{1,0:T(8,128)(2,1)} %param.11) | copy-start | bytes 3145732
  7.2 218.4 %copy-start.1 = (bf16[512,1024]{1,0:T(8,128)(2,1)S(1)}, bf16[512,1024]{1,0:T(8,128)(2,1)}, u32[]{:S(2)}) copy-start(bf16[512,1024]{1,0:T(8,128)(2,1)} %param.10) | copy-start | bytes 3145732
  7.2 218.4 %copy-start.3 = (f32[512]{0:T(512)S(1)}, f32[512]{0:T(512)}, u32[]{:S(2)}) copy-start(f32[512]{0:T(512)} %param.9) | copy-start | bytes 6148
  7.2 218.4 %copy-start.2 = (bf16[176,512]{1,0:T(8,128)(2,1)S(1)}, bf16[176,512]{1,0:T(8,128)(2,1)}, u32[]{:S(2)}) copy-start(bf16[176,512]{1,0:T(8,128)(2,1)} %param.7) | copy-start | bytes 540676
  7.2 106.0 %all-gather.3.cloned.1.call-start = ((), (), s32[]{:S(2)}) async-start(), calls=%async_computation.1 | async-start | bytes 11624448 | tf_op jit(solution)/shard_map/all_gather | solution.py:11
  7.9 217.6 %reduce-scatter.2.cloned.1.call-start = ((), (), s32[]{:S(2)}) async-start(), calls=%async_computation.2 | async-start | bytes 3244032 | tf_op jit(solution)/shard_map/reduce_scatter | solution.py:14
  121.7 218.3 %all-reduce.2.cloned.1.call-start = ((), (), s32[]{:S(2)}) async-start(), calls=%async_computation.3 | async-start | bytes 1441792 | tf_op jit(solution)/shard_map/psum | solution.py:18
  227.8 194.4 %all-gather.5.cloned.1.call-start = ((), (), s32[]{:S(2)}) async-start(), calls=%async_computation.4 | async-start | bytes 11894784 | tf_op jit(solution)/shard_map/all_gather | solution.py:22
Sparse Core Ops, SparseCore 0:
  9.8 103.3 all-gather.2
  121.8 103.6 reduce-scatter.1
  228.8 111.2 all-reduce.1
  343.4 78.7 all-gather.4
where the time goes:
time: 618 us; the launch traced here: 617 us
  waiting for transfers between devices  401 us (65%)
  blocking collectives  149 us (24%)
  matrix products  37.1 us (6%)
  other arithmetic  15.8 us (3%)
  between operations  13.8 us (2%)
    psum x1, waiting for transfers between devices, body(): embed_full = lax.psum(partial_embed, 'cent')  112 us
    all_gather x1, waiting for transfers between devices, body(): lax.all_gather(down_weight, 'dp', axis=1, tiled=True)  105 us
    reduce_scatter x1, waiting for transfers between devices, body(): lax.psum_scatter(partial_layer, 'cent', scatter_dimension=1, tiled=True)  104 us
    all_gather x1, waiting for transfers between devices, body(): gathered = lax.all_gather(scaled, 'dp', axis=0, tiled=True)  78.9 us
    pmax x1, blocking collectives, body(): row_max = lax.pmax(local_max, ('dp', 'cent'))  76.1 us
    psum x1, blocking collectives, body(): lax.psum(jnp.sum(jnp.exp(scores - row_max[:, None]), axis=1), ('dp', 'cen...  73.3 us
    dot_general x1, matrix products, body(): lax.dot_general(prob_low, gathered, (((0,), (0,)), ((), ())), preferred_e...  13.3 us
    dot_general x1, matrix products, body(): lax.dot_general(gathered, centroids, (((1,), (1,)), ((), ())), preferred_...  13.2 us
  transfers between devices with their start and end apart: 4, of which 4 were waited for; matrix products, arithmetic and copies ran while one was open for 0% of the time, Pallas kernels for 0%

commit v1 on v0

--- a/solution.py
+++ b/solution.py
@@ -8,7 +8,9 @@
 def body(hidden, residual, down_weight, gain, proj_weight, centroids):
     partial_layer = jnp.dot(
         hidden,
-        lax.all_gather(down_weight, "dp", axis=1, tiled=True),
+        jnp.concatenate(
+            lax.all_to_all(jnp.stack([down_weight] * lax.axis_size("dp")), "dp", 0, 0), axis=1
+        ),
         preferred_element_type=jnp.float32,
     )
     layer_out = lax.psum_scatter(partial_layer, "cent", scatter_dimension=1, tiled=True)

time: 618 us -> 792 us (1.28)
  blocking collectives: 149 us -> 407 us
  waiting for transfers between devices: 401 us -> 294 us
  local copies, waits for them, and re-layouts: 0.02 us -> 21.9 us
    all_to_all x0 -> x1, blocking collectives: none -> 257 us  [body(): lax.all_to_all(jnp.stack([down_weight] * lax.axis_size('dp')), 'dp', 0, 0)]
    all_gather x1 -> x0, waiting for transfers between devices: 105 us -> none  [body(): lax.all_gather(down_weight, 'dp', axis=1, tiled=True)]
    reshape x0 -> x1, local copies, waits for them, and re-layouts: none -> 15.1 us  [body(): jnp.concatenate(lax.all_to_all(jnp.stack([down_weight] * lax.axis_size('d...]
  transfers between devices with their start and end apart: 4 -> 3, of which waited for: 4 -> 3; matrix products, arithmetic and copies ran while one was open for 0% -> 0% of each run, Pallas kernels for 0% -> 0%
where the time goes in v1:
time: 792 us; the launch traced here: 791 us
  blocking collectives  407 us (51%)
  waiting for transfers between devices  294 us (37%)
  matrix products  38.7 us (5%)
  local copies, waits for them, and re-layouts  21.9 us (3%)
  other arithmetic  15.8 us (2%)
  between operations  13.8 us (2%)
    all_to_all x1, blocking collectives, body(): lax.all_to_all(jnp.stack([down_weight] * lax.axis_size('dp')), 'dp', 0, 0)  257 us
    psum x1, waiting for transfers between devices, body(): embed_full = lax.psum(partial_embed, 'cent')  112 us
    reduce_scatter x1, waiting for transfers between devices, body(): lax.psum_scatter(partial_layer, 'cent', scatter_dimension=1, tiled=True)  103 us
    all_gather x1, waiting for transfers between devices, body(): gathered = lax.all_gather(scaled, 'dp', axis=0, tiled=True)  78.9 us
    pmax x1, blocking collectives, body(): row_max = lax.pmax(local_max, ('dp', 'cent'))  76.1 us
    psum x1, blocking collectives, body(): lax.psum(jnp.sum(jnp.exp(scores - row_max[:, None]), axis=1), ('dp', 'cen...  73.3 us
  transfers between devices with their start and end apart: 3, of which 3 were waited for; matrix products, arithmetic and copies ran while one was open for 0% of the time, Pallas kernels for 0%

profile of v1, /device:TPU:1, one launch (start us, length us, event | category | flops | bytes accessed | tf_op | source)
XLA Modules:
  0.0 790.8 jit_solution(3884940150533967789)
XLA Ops:
  7.2 0.0 copy-start
  7.2 0.0 reduce-scatter.2.cloned.1.call-start
  7.2 6.8 stack.2
  14.0 257.3 %all_to_all.5 = bf16[32,1376,128]{2,1,0:T(8,128)(2,1)} all-to-all(bf16[32,1376,128]{2,1,0:T(8,128)(2,1)} %stack.2), channel_id=1, replica_groups=mesh['dp'=32,'cent'=8] {'dp'}, dimensions={0} | all-to-all | bytes 22544384 | tf_op jit(solution)/shard_map/all_to_all | solution.py:12
  271.3 0.0 copy-start.3
  271.3 15.1 %copy.9 = bf16[1376,32,128]{0,2,1:T(8,128)(2,1)} copy(bf16[1376,32,128]{2,0,1:T(8,128)(2,1)} %bitcast.9) | data formatting | bytes 22544384 | tf_op jit(solution)/shard_map/reshape | solution.py:11
  286.4 0.0 copy-start.2
  286.4 0.0 copy-start.4
  286.4 0.0 copy-start.5
  286.4 0.0 copy-done.3
  286.4 10.0 %fusion.11 = f32[176,4096]{1,0:T(8,128)} fusion(bf16[176,1376]{1,0:T(8,128)(2,1)S(1)} %copy-done.3, bf16[1376,4096]{0,1:T(8,128)(2,1)} %bitcast.8), kind=kOutput, calls=%fused_computation.17 | convolution fusion | flops 1983905792 | bytes 14640128 | tf_op jit(solution)/shard_map/dot_general | solution.py:9
  296.5 0.0 reduce-scatter.2.cloned.1.call-update
  296.5 0.0 all-reduce.2.cloned.1.call-start
  296.5 102.6 %reduce-scatter.2.cloned.1.call-done = f32[176,512]{1,0:T(8,128)} async-done(((f32[176,4096]{1,0:T(8,128)}), f32[176,512]{1,0:T(8,128)}) %reduce-scatter.2.cloned.1.call-update) | async-done | bytes 360464 | tf_op jit(solution)/shard_map/reduce_scatter | solution.py:16
  399.1 0.0 copy-done.2
  399.1 0.0 copy-done.4
  399.1 0.0 copy-done.5
  399.1 2.2 fusion.8
  401.3 0.0 all-reduce.2.cloned.1.call-update
  401.3 0.0 all-gather.2.cloned.1.call-start
  401.4 112.2 %all-reduce.2.cloned.1.call-done = f32[176,1024]{1,0:T(8,128)} async-done(((f32[176,1024]{1,0:T(8,128)}), f32[176,1024]{1,0:T(8,128)}) %all-reduce.2.cloned.1.call-update) | async-done | bytes 720912 | tf_op jit(solution)/shard_map/psum | solution.py:20
  513.6 1.2 multiply_reduce_fusion
  514.9 2.0 multiply_convert_fusion
  516.8 0.0 all-gather.2.cloned.1.call-update
  516.9 78.9 %all-gather.2.cloned.1.call-done = bf16[5632,1024]{1,0:T(8,128)(2,1)} async-done(((bf16[176,1024]{1,0:T(8,128)(2,1)}), bf16[5632,1024]{1,0:T(8,128)(2,1)}) %all-gather.2.cloned.1.call-update) | async-done | bytes 11534352 | tf_op jit(solution)/shard_map/all_gather | solution.py:24
  595.7 0.0 copy-done
  595.7 13.2 %fusion.10 = (f32[5632]{0:T(1024)S(1)}, f32[5632,512]{0,1:T(8,128)}) fusion(bf16[5632,1024]{1,0:T(8,128)(2,1)} %all-gather.2.cloned.1.call-done, bf16[512,1024]{1,0:T(8,128)(2,1)S(1)} %copy-done), kind=kOutput, calls=%fused_computation.16 | convolution fusion | flops 5911341568 | bytes 24139776 | tf_op jit(solution)/shard_map/dot_general | solution.py:27
  608.9 76.1 %pmax.7 = f32[5632]{0:T(1024)S(1)} all-reduce(f32[5632]{0:T(1024)S(1)} %get-tuple-element.2), channel_id=1, replica_groups=mesh['dp'=32,'cent'=8] {'dp','cent'}, use_global_device_ids=true, to_apply=%region_4.0 | all-reduce | flops 5632 | bytes 45056 | tf_op jit(solution)/shard_map/pmax | solution.py:33
  685.0 6.0 exponential_reduce_fusion
  691.0 73.3 %psum.15 = f32[5632]{0:T(1024)S(1)} all-reduce(f32[5632]{0:T(1024)S(1)} %exponential_reduce_fusion), channel_id=1, replica_groups=mesh['dp'=32,'cent'=8] {'dp','cent'}, use_global_device_ids=true, to_apply=%region_6.0 | all-reduce | flops 5632 | bytes 45056 | tf_op jit(solution)/shard_map/psum | solution.py:34
  764.3 6.0 fusion
  770.3 0.6 broadcast_multiply_fusion
  770.9 0.0 copy-start.1
  770.9 13.3 %fusion.5 = f32[512,1024]{1,0:T(8,128)} fusion(bf16[5632,1024]{1,0:T(8,128)(2,1)} %all-gather.2.cloned.1.call-done, f32[5632,512]{0,1:T(8,128)} %get-tuple-element.3, f32[5632]{0:T(1024)S(1)} %log_add_fusion), kind=kOutput, calls=%fused_computation.7 | convolution fusion | flops 5911871488 | bytes 25188352 | tf_op jit(solution)/shard_map/dot_general | solution.py:40
  784.2 0.0 copy-done.1
  (2 shorter events, 0.0 us)
Async XLA Ops:
  7.2 588.6 %copy-start = (bf16[512,1024]{1,0:T(8,128)(2,1)S(1)}, bf16[512,1024]{1,0:T(8,128)(2,1)}, u32[]{:S(2)}) copy-start(bf16[512,1024]{1,0:T(8,128)(2,1)} %param.11) | copy-start | bytes 3145732
  7.2 391.9 %reduce-scatter.2.cloned.1.call-start = ((), (), s32[]{:S(2)}) async-start(), calls=%async_computation.2 | async-start | bytes 3244032 | tf_op jit(solution)/shard_map/reduce_scatter | solution.py:16
  271.3 15.1 %copy-start.3 = (bf16[176,1376]{1,0:T(8,128)(2,1)S(1)}, bf16[176,1376]{1,0:T(8,128)(2,1)}, u32[]{:S(2)}) copy-start(bf16[176,1376]{1,0:T(8,128)(2,1)} %param.6) | copy-start | bytes 1453060
  286.4 112.7 %copy-start.2 = (bf16[512,1024]{1,0:T(8,128)(2,1)S(1)}, bf16[512,1024]{1,0:T(8,128)(2,1)}, u32[]{:S(2)}) copy-start(bf16[512,1024]{1,0:T(8,128)(2,1)} %param.10) | copy-start | bytes 3145732
  286.4 112.7 %copy-start.4 = (bf16[176,512]{1,0:T(8,128)(2,1)S(1)}, bf16[176,512]{1,0:T(8,128)(2,1)}, u32[]{:S(2)}) copy-start(bf16[176,512]{1,0:T(8,128)(2,1)} %param.7) | copy-start | bytes 540676
  286.4 112.7 %copy-start.5 = (f32[512]{0:T(512)S(1)}, f32[512]{0:T(512)}, u32[]{:S(2)}) copy-start(f32[512]{0:T(512)} %param.9) | copy-start | bytes 6148
  296.5 217.2 %all-reduce.2.cloned.1.call-start = ((), (), s32[]{:S(2)}) async-start(), calls=%async_computation.3 | async-start | bytes 1441792 | tf_op jit(solution)/shard_map/psum | solution.py:20
  401.3 194.4 %all-gather.2.cloned.1.call-start = ((), (), s32[]{:S(2)}) async-start(), calls=%async_computation.4 | async-start | bytes 11894784 | tf_op jit(solution)/shard_map/all_gather | solution.py:24
  770.9 13.3 %copy-start.1 = (bf16[512,1024]{1,0:T(8,128)(2,1)S(1)}, bf16[512,1024]{1,0:T(8,128)(2,1)}, u32[]{:S(2)}) copy-start(bf16[512,1024]{1,0:T(8,128)(2,1)} %param.11) | copy-start | bytes 3145732
Sparse Core Ops, SparseCore 0:
  296.6 102.4 reduce-scatter.1
  402.3 111.2 all-reduce.1
  517.0 78.7 all-gather.1
